TPU v7x, 32 devices: a whole 2x2x4 slice. The times are simulated.
32 devices in a mesh: dp: 8 (over z, x), ctx: 4 (over y, core).
Axes of the slice: x: 2, y: 2, z: 4, core: 2. Of those that a mesh axis runs over, the one named last changes fastest.
Arguments:
- tokens: bfloat16 [32, 2560, 1280], P('dp', 'ctx'), may hold values from -64 to 64
- router: bfloat16 [1280, 64], replicated, may hold values from -1 to 1
- expert_up: bfloat16 [32, 1280, 2560], P(('dp', 'ctx')), may hold values from -0.5 to 0.5
- expert_down: bfloat16 [32, 2560, 1280], P(('dp', 'ctx')), may hold values from -0.25 to 0.25
Outputs:
- mixed: bfloat16 [32, 2560, 1280], P('dp', 'ctx')
All inputs are finite; a program needn't handle non-finite values.
Results may differ from a plain program's by a relative error of at most 0.015.
Values may be sent and summed in bfloat16 or wider, within the bound.
A program may use at most 128 MiB of HBM per device.

v0:
```python
import jax
import jax.numpy as jnp
from jax import lax
from jax.sharding import PartitionSpec as P


def merged(x, axis, combine):
    everything = jax.tree.map(lambda part: lax.all_gather(part, axis), x)
    initial = jax.tree.map(lambda part: part[0], everything)

    def step(k, so_far):
        return combine(so_far, jax.tree.map(lambda part: part[k], everything))

    return lax.fori_loop(1, lax.axis_size(axis), step, initial)


def merge_stats(earlier, later):
    highest = jnp.maximum(earlier[0], later[0])
    return (
        highest,
        earlier[1] * jnp.exp(earlier[0] - highest) + later[1] * jnp.exp(later[0] - highest),
    )


def expert_rows(grouped, up_matrix, down_matrix):
    feature = grouped.shape[-1]
    flat = grouped.reshape(-1, feature)
    hidden = jax.nn.gelu(
        jnp.dot(flat, up_matrix, preferred_element_type=jnp.float32), approximate=False
    ).astype(jnp.bfloat16)
    produced = jnp.dot(hidden, down_matrix, preferred_element_type=jnp.float32).astype(jnp.bfloat16)
    return produced.reshape(grouped.shape)


def shards(tokens, router, expert_up, expert_down):
    clip_dev, tok_dev, feature = tokens.shape
    dp_size = lax.axis_size("dp")
    ctx_size = lax.axis_size("ctx")
    slot_total = router.shape[1]
    per_expert = slot_total // (dp_size * ctx_size)
    ordered = (
        router.reshape(feature, dp_size, ctx_size, per_expert)
        .transpose(0, 2, 1, 3)
        .reshape(feature, slot_total)
    )
    logits = jnp.einsum("ctd,dj->ctj", tokens, ordered, preferred_element_type=jnp.float32)
    local_max = jnp.max(logits, axis=1)
    exponent = jnp.exp(logits - local_max[:, None, :])
    column_max, column_sum = merged((local_max, jnp.sum(exponent, axis=1)), "ctx", merge_stats)
    exponent = exponent * jnp.exp(local_max - column_max)[:, None, :]
    dispatch = (exponent / column_sum[:, None, :]).astype(jnp.bfloat16)
    row_max = jnp.max(logits, axis=2)
    row_exp = jnp.exp(logits - row_max[:, :, None])
    combine = (row_exp / jnp.sum(row_exp, axis=2)[:, :, None]).astype(jnp.bfloat16)
    up_matrix = expert_up[0]
    down_matrix = expert_down[0]
    split_dispatch = dispatch.reshape(clip_dev, tok_dev, ctx_size, dp_size, per_expert)
    partial_value = jnp.einsum(
        "ctabs,ctd->cbasd", split_dispatch, tokens, preferred_element_type=jnp.float32
    ).astype(jnp.bfloat16)
    grouped = partial_value.reshape(clip_dev, dp_size * ctx_size, per_expert, feature)
    received = lax.all_to_all(grouped, ("dp", "ctx"), split_axis=1, concat_axis=1, tiled=True)
    amount = received.shape[0]
    blocks = received.astype(jnp.float32).reshape(amount, dp_size, ctx_size, per_expert, feature)
    results = expert_rows(jnp.sum(blocks, axis=2).astype(jnp.bfloat16), up_matrix, down_matrix)
    returned = lax.all_to_all(results, "dp", split_axis=1, concat_axis=1, tiled=True)
    returned = returned.reshape(clip_dev, dp_size * per_expert, feature)
    mixed = jnp.einsum(
        "ctj,cjd->ctd",
        combine,
        lax.all_gather(returned, "ctx", axis=1, tiled=True),
        preferred_element_type=jnp.float32,
    )
    return mixed.astype(jnp.bfloat16)


def solution(mesh):
    in_specs = (
        P("dp", "ctx", None),
        P(),
        P(("dp", "ctx"), None, None),
        P(("dp", "ctx"), None, None),
    )
    out_specs = P("dp", "ctx", None)
    return jax.shard_map(shards, mesh=mesh, in_specs=in_specs, out_specs=out_specs, check_vma=False)
```

profile of v0, /device:TPU:0, one launch (start us, length us, event | category | flops | bytes accessed | tf_op | source)
XLA Modules:
  0.0 80.9 jit_solution(9452041933624076778)
XLA Ops:
  0.0 1.0 %reshape.38 = bf16[1280,8,4,2]{0,3,2,1:T(2,128)(2,1)S(1)} reshape(bf16[1280,64]{0,1:T(8,128)(2,1)} %param.7) | data formatting | bytes 327680 | tf_op jit(solution)/shard_map/reshape | solution.py:42
  1.0 0.1 copy.22
  1.1 0.1 reshape.60
  1.2 5.0 %fusion.98 = (f32[4,64]{1,0:T(4,128)S(1)}, f32[4,640,64]{1,2,0:T(8,128)S(1)}) fusion(bf16[4,640,1280]{2,1,0:T(8,128)(2,1)} %param.6, bf16[1280,64,1]{0,1,2:T(8,128)(2,1)S(1)} %reshape.60), kind=kOutput, calls=%fused_computation.108 | convolution fusion | flops 419593984 | bytes 7373824 | tf_op jit(solution)/shard_map/ctd,dj->ctj/dot_general | solution.py:46
  6.2 0.3 fusion.34
  6.5 6.2 %all-gather.3 = f32[4,4,64]{2,1,0:T(4,128)S(1)} all-gather(f32[1,4,64]{2,1,0:T(4,128)S(1)} %bitcast.63), channel_id=3, replica_groups=mesh['dp'=8,'ctx'=4] {'ctx'}, dimensions={0}, use_global_device_ids=true | all-gather | bytes 5120 | tf_op jit(solution)/shard_map/all_gather | solution.py:8
  12.7 5.5 %all-gather.2 = f32[4,4,64]{2,1,0:T(4,128)S(1)} all-gather(f32[1,4,64]{2,1,0:T(4,128)S(1)} %bitcast.62), channel_id=2, replica_groups=mesh['dp'=8,'ctx'=4] {'ctx'}, dimensions={0}, use_global_device_ids=true | all-gather | bytes 5120 | tf_op jit(solution)/shard_map/all_gather | solution.py:8
  18.1 0.1 while.17
  18.3 0.2 divide_convert_fusion
  18.5 0.1 reshape.40
  18.6 4.1 %fusion.12 = bf16[4,8,4,2,1280]{4,1,3,2,0:T(8,128)(2,1)S(1)} fusion(bf16[4,640,1280]{2,1,0:T(8,128)(2,1)} %param.6, bf16[4,640,4,8,2]{1,4,3,2,0:T(2,128)(2,1)S(1)} %reshape.40), kind=kOutput, calls=%fused_computation.14 | convolution fusion | flops 419758080 | bytes 7536640 | tf_op jit(solution)/shard_map/ctabs,ctd->cbasd/dot_general | solution.py:58
  22.7 0.5 copy.30
  23.2 23.8 %all_to_all.10 = bf16[4,32,2,1280]{3,2,0,1:T(2,128)(2,1)S(1)} all-to-all(bf16[4,32,2,1280]{3,2,0,1:T(2,128)(2,1)S(1)} %bitcast.60), channel_id=1, replica_groups=mesh['dp'=8,'ctx'=4] {'dp','ctx'}, dimensions={1} | all-to-all | bytes 1310720 | tf_op jit(solution)/shard_map/all_to_all | solution.py:62
  47.0 0.7 bitcast_reduce_fusion
  47.7 0.1 copy.26
  47.8 0.1 convert_element_type.40
  47.9 8.0 %fusion.15 = bf16[64,1280]{1,0:T(8,128)(2,1)S(1)} fusion(bf16[1,2560,1280]{2,1,0:T(8,128)(2,1)} %param.9, bf16[64,1280]{1,0:T(8,128)(2,1)S(1)} %convert_element_type.40, bf16[1,1280,2560]{2,1,0:T(8,128)(2,1)} %param.8), kind=kOutput, calls=%fused_computation.15 | convolution fusion | flops 849592320 | bytes 13434880 | tf_op jit(solution)/shard_map/dot_general | solution.py:31
  55.9 0.1 reshape.44
  56.0 0.8 copy.27
  56.8 3.4 %all-to-all-start.1 = ((bf16[4,8,2,1280]{3,2,0,1:T(2,128)(2,1)}), bf16[4,8,2,1280]{3,2,0,1:T(2,128)(2,1)S(1)}, u32[]{:S(2)}, u32[]{:S(2)}) async-start(bf16[4,8,2,1280]{3,2,0,1:T(2,128)(2,1)} %copy.27), calls=%async_computation.1 | async-start | bytes 327680 | tf_op jit(solution)/shard_map/all_to_all | solution.py:66
  60.2 0.2 fusion.99
  60.3 7.7 %all-to-all-done.1 = bf16[4,8,2,1280]{3,2,0,1:T(2,128)(2,1)S(1)} async-done(((bf16[4,8,2,1280]{3,2,0,1:T(2,128)(2,1)}), bf16[4,8,2,1280]{3,2,0,1:T(2,128)(2,1)S(1)}, u32[]{:S(2)}, u32[]{:S(2)}) %all-to-all-start.1) | async-done | bytes 163872 | tf_op jit(solution)/shard_map/all_to_all | solution.py:66
  68.1 0.1 copy.28
  68.2 0.1 reshape.45
  68.3 7.9 %all_gather.19 = bf16[4,64,1280]{2,1,0:T(8,128)(2,1)S(1)} all-gather(bf16[4,16,1280]{2,1,0:T(8,128)(2,1)S(1)} %reshape.45), channel_id=1, replica_groups=mesh['dp'=8,'ctx'=4] {'ctx'}, dimensions={1}, use_global_device_ids=true | all-gather | bytes 819200 | tf_op jit(solution)/shard_map/all_gather | solution.py:71
  76.2 4.7 %convolution_convert_fusion = bf16[4,640,1280]{2,1,0:T(8,128)(2,1)} fusion(bf16[4,64,1280]{2,1,0:T(8,128)(2,1)S(1)} %all_gather.19, f32[4,640]{1,0:T(4,128)S(1)} %fusion.99, f32[4,640,64]{1,2,0:T(8,128)S(1)} %get-tuple-element.153), kind=kOutput, calls=%fused_computation.12 | convolution fusion | flops 423201344 | bytes 7874560 | tf_op jit(solution)/shard_map/ctj,cjd->ctd/dot_general | solution.py:68
  (6 shorter events, 0.1 us)
Async XLA Ops:
  56.8 11.3 %all-to-all-start.1 = ((bf16[4,8,2,1280]{3,2,0,1:T(2,128)(2,1)}), bf16[4,8,2,1280]{3,2,0,1:T(2,128)(2,1)S(1)}, u32[]{:S(2)}, u32[]{:S(2)}) async-start(bf16[4,8,2,1280]{3,2,0,1:T(2,128)(2,1)} %copy.27), calls=%async_computation.1 | async-start | bytes 327680 | tf_op jit(solution)/shard_map/all_to_all | solution.py:66
where the time goes:
time: 81.2 us; the launch traced here: 80.9 us
  blocking collectives  43.4 us (53%)
  matrix products  21.8 us (27%)
  waiting for transfers between devices  7.72 us (10%)
  starting transfers between devices  3.42 us (4%)
  local copies, waits for them, and re-layouts  3 us (4%)
  other arithmetic  1.36 us (2%)
    all_to_all x1, blocking collectives, shards(): lax.all_to_all(grouped, ('dp', 'ctx'), split_axis=1, concat_axis=1, tiled...  23.8 us
    all_gather x2, blocking collectives, merged(): everything = jax.tree.map(lambda part: lax.all_gather(part, axis), x)  11.7 us
    dot_general x1, matrix products, expert_rows(): jnp.dot(hidden, down_matrix, preferred_element_type=jnp.float32)  8.01 us
    all_gather x1, blocking collectives, shards(): lax.all_gather(returned, 'ctx', axis=1, tiled=True)  7.9 us
    all_to_all x1, waiting for transfers between devices, shards(): lax.all_to_all(results, 'dp', split_axis=1, concat_axis=1, tiled=True)  7.72 us
    dot_general x1, matrix products, shards(): jnp.einsum('ctd,dj->ctj', tokens, ordered, preferred_element_type=jnp.flo...  5.03 us
    dot_general x1, matrix products, shards(): jnp.einsum('ctj,cjd->ctd', combine, lax.all_gather(returned, 'ctx', axis=...  4.72 us
    dot_general x1, matrix products, shards(): jnp.einsum('ctabs,ctd->cbasd', split_dispatch, tokens, preferred_element_...  4.08 us
  transfers between devices with their start and end apart: 1, of which 1 were waited for; matrix products, arithmetic and copies ran while one was open for 0% of the time, Pallas kernels for 0%

commit v1 on v0

--- a/solution.py
+++ b/solution.py
@@ -65,12 +65,20 @@
     results = expert_rows(jnp.sum(blocks, axis=2).astype(jnp.bfloat16), up_matrix, down_matrix)
     returned = lax.all_to_all(results, "dp", split_axis=1, concat_axis=1, tiled=True)
     returned = returned.reshape(clip_dev, dp_size * per_expert, feature)
-    mixed = jnp.einsum(
-        "ctj,cjd->ctd",
-        combine,
-        lax.all_gather(returned, "ctx", axis=1, tiled=True),
-        preferred_element_type=jnp.float32,
-    )
+    size, here, rows = (lax.axis_size("ctx"), lax.axis_index("ctx"), returned.shape[1])
+    upward = [(i, (i + 1) % size) for i in range(size)]
+    current, running = (returned, None)
+    for lap in range(size):
+        coming = lax.ppermute(current, "ctx", upward) if lap < size - 1 else None
+        update = jnp.einsum(
+            "ctj,cjd->ctd",
+            lax.dynamic_slice_in_dim(combine, (here - lap) % size * rows, current.shape[1], axis=2),
+            current,
+            preferred_element_type=jnp.float32,
+        )
+        running = update if running is None else running + update
+        current = coming
+    mixed = running
     return mixed.astype(jnp.bfloat16)
 
 

time: 81.2 us -> 106 us (1.31)
  matrix products: 21.8 us -> 53.1 us
  blocking collectives: 43.4 us -> 35.5 us
  starting transfers between devices: 3.42 us -> 5.1 us
    dot_general x1 -> x4, matrix products: 4.72 us -> 36 us  [shards(): jnp.einsum('ctj,cjd->ctd', lax.dynamic_slice_in_dim(combine, (here - lap)...]
    all_gather x1 -> x0, blocking collectives: 7.9 us -> none  [shards(): lax.all_gather(returned, 'ctx', axis=1, tiled=True)]
    ppermute x0 -> x3, starting transfers between devices: none -> 1.68 us  [shards(): coming = lax.ppermute(current, 'ctx', upward) if lap < size - 1 else None]
  transfers between devices with their start and end apart: 1 -> 4, of which waited for: 1 -> 1; matrix products, arithmetic and copies ran while one was open for 0% -> 20% of each run, Pallas kernels for 0% -> 0%
where the time goes in v1:
time: 106 us
  matrix products  53.1 us (50%)
  blocking collectives  35.5 us (33%)
  waiting for transfers between devices  6.69 us (6%)
  starting transfers between devices  5.1 us (5%)
  local copies, waits for them, and re-layouts  3 us (3%)
  other arithmetic  2.31 us (2%)
    dot_general x4, matrix products, shards(): jnp.einsum('ctj,cjd->ctd', lax.dynamic_slice_in_dim(combine, (here - lap)...  36 us
    all_to_all x1, blocking collectives, shards(): lax.all_to_all(grouped, ('dp', 'ctx'), split_axis=1, concat_axis=1, tiled...  23.8 us
    all_gather x2, blocking collectives, merged(): everything = jax.tree.map(lambda part: lax.all_gather(part, axis), x)  11.7 us
    dot_general x1, matrix products, expert_rows(): jnp.dot(hidden, down_matrix, preferred_element_type=jnp.float32)  8.01 us
    all_to_all x1, waiting for transfers between devices, shards(): lax.all_to_all(results, 'dp', split_axis=1, concat_axis=1, tiled=True)  6.68 us
    dot_general x1, matrix products, shards(): jnp.einsum('ctd,dj->ctj', tokens, ordered, preferred_element_type=jnp.flo...  5.02 us
    dot_general x1, matrix products, shards(): jnp.einsum('ctabs,ctd->cbasd', split_dispatch, tokens, preferred_element_...  4.08 us
    all_to_all x1, starting transfers between devices, shards(): lax.all_to_all(results, 'dp', split_axis=1, concat_axis=1, tiled=True)  3.42 us
  transfers between devices with their start and end apart: 4, of which 1 were waited for; matrix products, arithmetic and copies ran while one was open for 20% of the time, Pallas kernels for 0%

profile of v1, /device:TPU:0, one launch (start us, length us, event | category | flops | bytes accessed | tf_op | source)
XLA Modules:
  0.0 106.0 jit_solution(17280990405096737258)
XLA Ops:
  0.0 1.0 reshape.38
  1.0 0.1 copy.22
  1.1 0.1 reshape.60
  1.2 5.0 %fusion.107 = (f32[4,64]{1,0:T(4,128)S(1)}, f32[4,640,64]{1,2,0:T(8,128)S(1)}) fusion(bf16[4,640,1280]{2,1,0:T(8,128)(2,1)} %param.6, bf16[1280,64,1]{0,1,2:T(8,128)(2,1)S(1)} %reshape.60), kind=kOutput, calls=%fused_computation.117 | convolution fusion | flops 419593984 | bytes 7373824 | tf_op jit(solution)/shard_map/ctd,dj->ctj/dot_general | solution.py:46
  6.2 0.3 fusion.34
  6.5 6.2 %all-gather.3 = f32[4,4,64]{2,1,0:T(4,128)S(1)} all-gather(f32[1,4,64]{2,1,0:T(4,128)S(1)} %bitcast.65), channel_id=3, replica_groups=mesh['dp'=8,'ctx'=4] {'ctx'}, dimensions={0}, use_global_device_ids=true | all-gather | bytes 5120 | tf_op jit(solution)/shard_map/all_gather | solution.py:8
  12.7 5.5 %all-gather.2 = f32[4,4,64]{2,1,0:T(4,128)S(1)} all-gather(f32[1,4,64]{2,1,0:T(4,128)S(1)} %bitcast.64), channel_id=2, replica_groups=mesh['dp'=8,'ctx'=4] {'ctx'}, dimensions={0}, use_global_device_ids=true | all-gather | bytes 5120 | tf_op jit(solution)/shard_map/all_gather | solution.py:8
  18.1 0.1 while.17
  18.2 0.2 divide_convert_fusion
  18.5 0.1 reshape.40
  18.6 4.1 %fusion.12 = bf16[4,8,4,2,1280]{4,1,3,2,0:T(8,128)(2,1)S(1)} fusion(bf16[4,640,1280]{2,1,0:T(8,128)(2,1)} %param.6, bf16[4,640,4,8,2]{1,4,3,2,0:T(2,128)(2,1)S(1)} %reshape.40), kind=kOutput, calls=%fused_computation.14 | convolution fusion | flops 419758080 | bytes 7536640 | tf_op jit(solution)/shard_map/ctabs,ctd->cbasd/dot_general | solution.py:58
  22.7 0.5 copy.30
  23.2 23.8 %all_to_all.10 = bf16[4,32,2,1280]{3,2,0,1:T(2,128)(2,1)S(1)} all-to-all(bf16[4,32,2,1280]{3,2,0,1:T(2,128)(2,1)S(1)} %bitcast.62), channel_id=1, replica_groups=mesh['dp'=8,'ctx'=4] {'dp','ctx'}, dimensions={1} | all-to-all | bytes 1310720 | tf_op jit(solution)/shard_map/all_to_all | solution.py:62
  47.0 0.7 bitcast_reduce_fusion
  47.7 0.1 copy.26
  47.8 0.1 convert_element_type.40
  47.9 8.0 %fusion.15 = bf16[64,1280]{1,0:T(8,128)(2,1)S(1)} fusion(bf16[1,2560,1280]{2,1,0:T(8,128)(2,1)} %param.9, bf16[64,1280]{1,0:T(8,128)(2,1)S(1)} %convert_element_type.40, bf16[1,1280,2560]{2,1,0:T(8,128)(2,1)} %param.8), kind=kOutput, calls=%fused_computation.15 | convolution fusion | flops 849592320 | bytes 13434880 | tf_op jit(solution)/shard_map/dot_general | solution.py:31
  55.9 0.1 reshape.44
  56.0 0.8 copy.27
  56.8 3.4 %all-to-all-start.1 = ((bf16[4,8,2,1280]{3,2,0,1:T(2,128)(2,1)}), bf16[4,8,2,1280]{3,2,0,1:T(2,128)(2,1)S(1)}, u32[]{:S(2)}, u32[]{:S(2)}) async-start(bf16[4,8,2,1280]{3,2,0,1:T(2,128)(2,1)} %copy.27), calls=%async_computation.1 | async-start | bytes 327680 | tf_op jit(solution)/shard_map/all_to_all | solution.py:66
  60.2 1.0 fusion.108
  61.3 0.1 divide_convert_fusion.1
  61.4 6.7 %all-to-all-done.1 = bf16[4,8,2,1280]{3,2,0,1:T(2,128)(2,1)S(1)} async-done(((bf16[4,8,2,1280]{3,2,0,1:T(2,128)(2,1)}), bf16[4,8,2,1280]{3,2,0,1:T(2,128)(2,1)S(1)}, u32[]{:S(2)}, u32[]{:S(2)}) %all-to-all-start.1) | async-done | bytes 163872 | tf_op jit(solution)/shard_map/all_to_all | solution.py:66
  68.1 0.1 copy.28
  68.2 0.1 reshape.45
  68.2 0.1 collective-permute-start
  68.3 6.6 %fusion.71 = f32[4,640,1280]{2,1,0:T(8,128)} fusion(bf16[4,16,1280]{2,1,0:T(8,128)(2,1)S(1)} %reshape.45, bf16[4,640,64]{1,2,0:T(8,128)(2,1)S(1)} %divide_convert_fusion.1, s32[]{:T(128)S(6)} %select_n.43), kind=kOutput, calls=%fused_computation.78 | convolution fusion | flops 104857600 | bytes 13352964 | tf_op jit(solution)/shard_map/ctj,cjd->ctd/dot_general | solution.py:73
  74.9 1.6 %collective-permute-start.1 = (bf16[4,16,1280]{2,1,0:T(8,128)(2,1)S(1)}, bf16[4,16,1280]{2,1,0:T(8,128)(2,1)S(1)}, u32[]{:S(2)}, u32[]{:S(2)}) collective-permute-start(bf16[4,16,1280]{2,1,0:T(8,128)(2,1)S(1)} %collective-permute-done), channel_id=1, source_target_pairs={{0,1},{1,2},{2,3},{3,0},{4,5},{5,6},{6,7},{7,4},{8,9},{9,10},{10,1... | collective-permute-start | bytes 491528 | tf_op jit(solution)/shard_map/ppermute | solution.py:72
  76.5 6.6 %fusion.69 = f32[4,640,1280]{2,1,0:T(8,128)} fusion(bf16[4,16,1280]{2,1,0:T(8,128)(2,1)S(1)} %collective-permute-done, bf16[4,640,64]{1,2,0:T(8,128)(2,1)S(1)} %divide_convert_fusion.1, s32[]{:T(128)S(6)} %select_n.45), kind=kOutput, calls=%fused_computation.76 | convolution fusion | flops 104857600 | bytes 13352964 | tf_op jit(solution)/shard_map/ctj,cjd->ctd/dot_general | solution.py:73
  83.2 0.0 collective-permute-start.2
  83.2 6.6 %fusion.67 = f32[4,640,1280]{2,1,0:T(8,128)} fusion(bf16[4,16,1280]{2,1,0:T(8,128)(2,1)S(1)} %collective-permute-done.1, bf16[4,640,64]{1,2,0:T(8,128)(2,1)S(1)} %divide_convert_fusion.1, s32[]{:T(128)S(6)} %select_n.47), kind=kOutput, calls=%fused_computation.74 | convolution fusion | flops 104857600 | bytes 13352964 | tf_op jit(solution)/shard_map/ctj,cjd->ctd/dot_general | solution.py:73
  89.8 16.2 %add_convert_fusion = bf16[4,640,1280]{2,1,0:T(8,128)(2,1)} fusion(f32[4,640,1280]{2,1,0:T(8,128)} %fusion.67, f32[4,640,1280]{2,1,0:T(8,128)} %fusion.71, f32[4,640,1280]{2,1,0:T(8,128)} %fusion.69, bf16[4,16,1280]{2,1,0:T(8,128)(2,1)S(1)} %collective-permute-done.2, bf16[4,640,64]{1,2,0:T(8,128)(2,1)S(1)} %divide_convert_fusion.1, s32[]{:T(128)S(6)} %select_n.49), kind=kOutput, calls=%fused_computation.6 | convolution fusion | flops 117964800 | bytes 46120964 | tf_op jit(solution)/shard_map/ctj,cjd->ctd/dot_general | solution.py:73
  (9 shorter events, 0.1 us)
Async XLA Ops:
  56.8 11.3 %all-to-all-start.1 = ((bf16[4,8,2,1280]{3,2,0,1:T(2,128)(2,1)}), bf16[4,8,2,1280]{3,2,0,1:T(2,128)(2,1)S(1)}, u32[]{:S(2)}, u32[]{:S(2)}) async-start(bf16[4,8,2,1280]{3,2,0,1:T(2,128)(2,1)} %copy.27), calls=%async_computation.1 | async-start | bytes 327680 | tf_op jit(solution)/shard_map/all_to_all | solution.py:66
  68.2 6.7 %collective-permute-start = (bf16[4,16,1280]{2,1,0:T(8,128)(2,1)S(1)}, bf16[4,16,1280]{2,1,0:T(8,128)(2,1)S(1)}, u32[]{:S(2)}, u32[]{:S(2)}) collective-permute-start(bf16[4,16,1280]{2,1,0:T(8,128)(2,1)S(1)} %reshape.45), channel_id=1, source_target_pairs={{0,1},{1,2},{2,3},{3,0},{4,5},{5,6},{6,7},{7,4},{8,9},{9,10},{10,1... | collective-permute-start | bytes 491528 | tf_op jit(solution)/shard_map/ppermute | solution.py:72
  74.9 8.2 %collective-permute-start.1 = (bf16[4,16,1280]{2,1,0:T(8,128)(2,1)S(1)}, bf16[4,16,1280]{2,1,0:T(8,128)(2,1)S(1)}, u32[]{:S(2)}, u32[]{:S(2)}) collective-permute-start(bf16[4,16,1280]{2,1,0:T(8,128)(2,1)S(1)} %collective-permute-done), channel_id=1, source_target_pairs={{0,1},{1,2},{2,3},{3,0},{4,5},{5,6},{6,7},{7,4},{8,9},{9,10},{10,1... | collective-permute-start | bytes 491528 | tf_op jit(solution)/shard_map/ppermute | solution.py:72
  83.2 6.6 %collective-permute-start.2 = (bf16[4,16,1280]{2,1,0:T(8,128)(2,1)S(1)}, bf16[4,16,1280]{2,1,0:T(8,128)(2,1)S(1)}, u32[]{:S(2)}, u32[]{:S(2)}) collective-permute-start(bf16[4,16,1280]{2,1,0:T(8,128)(2,1)S(1)} %collective-permute-done.1), channel_id=1, source_target_pairs={{0,1},{1,2},{2,3},{3,0},{4,5},{5,6},{6,7},{7,4},{8,9},{9,10},{10,1... | collective-permute-start | bytes 491528 | tf_op jit(solution)/shard_map/ppermute | solution.py:72
